TPU v7x, 512 devices: a whole 4x4x16 slice. The times are simulated.
512 devices in a mesh: az: 16 (over z_hi, x, core), curve: 32 (over z_lo, y).
Axes of the slice: x: 4, y: 4, z: 16 (z_hi: 2, z_lo: 8; z = z_hi * 8 + z_lo), core: 2. Of those that a mesh axis runs over, the one named last changes fastest.
Arguments:
- fields: float32 [2, 256, 16, 4096], P(None, 'az', None, 'curve'), may hold values from -6 to 6
- impedance: float32 [2, 256, 4096], P(None, 'az', 'curve'), may hold values from 0.25 to 1.5
- tile_data: bfloat16 [256, 32, 3, 2, 128, 128], P('az', 'curve'), may hold values from -0.21875 to 0.21875
- tile_cols: int32 [256, 32, 3], P('az', 'curve'), may hold values from 0 to 31, as said below
- tile_count: int32 [256, 32], P('az', 'curve'), may hold values from 1 to 3
Outputs:
- applied: float32 [2, 256, 16, 4096], P(None, 'az', None, 'curve')
Inputs may be any that keep to these rules, and one draw needn't show every extreme that they name: `tile_cols`: for every mode and block row the 3 entries are distinct blocks lying within one block of the row's own block along the closed curve, indices taken modulo 32; only the first tile_count entries are used.
All inputs are finite; a program needn't handle non-finite values.
Results may differ from a plain program's by a relative error of at most 0.0021.
Values may be sent and summed in bfloat16 or wider, within the bound.
A program may use at most 64 MiB of HBM per device.

v0:
```python
import math

import jax
import jax.numpy as jnp
from jax import lax
from jax.sharding import PartitionSpec as P


def extended_2(x, sides, width):
    for axis, dim in sides:
        size, length = (lax.axis_size(axis), x.shape[dim])
        up = [(i, (i + 1) % size) for i in range(size)]
        down = [(j, i) for i, j in up]
        last = lax.slice_in_dim(x, length - width, length, axis=dim)
        first = lax.slice_in_dim(x, 0, width, axis=dim)
        before = lax.ppermute(last, axis, up)
        after = lax.ppermute(first, axis, down)
        x = jnp.concatenate([before, x, after], axis=dim)
    return x


def phase_table(left_index, right_index, period):
    product = jnp.mod(left_index[:, None] * right_index[None, :], period)
    angles = 2.0 * math.pi / period * product.astype(jnp.float32)
    return (jnp.cos(angles), jnp.sin(angles))


def exact_dot(left, right):
    return jnp.dot(left, right, precision=lax.Precision.HIGHEST, preferred_element_type=jnp.float32)


def forward_mix(cosine_table, sine_table, real_part, imag_part):
    real_out = exact_dot(cosine_table, real_part) + exact_dot(sine_table, imag_part)
    imag_out = exact_dot(cosine_table, imag_part) - exact_dot(sine_table, real_part)
    return (real_out, imag_out)


def inverse_mix(cosine_table, sine_table, real_part, imag_part):
    real_out = exact_dot(cosine_table, real_part) - exact_dot(sine_table, imag_part)
    imag_out = exact_dot(cosine_table, imag_part) + exact_dot(sine_table, real_part)
    return (real_out, imag_out)


def tile_apply(matrices, values):
    return jnp.einsum("mbtpq,mrbtq->mrbp", matrices, values, preferred_element_type=jnp.float32)


def on_device(fields, impedance, tile_data, tile_cols, tile_count):
    azimuth_devices = lax.axis_size("az")
    local_phi = fields.shape[1]
    period = local_phi * azimuth_devices
    rhs_count = fields.shape[2]
    node_count = fields.shape[3]
    flat_width = rhs_count * node_count
    block_size = tile_data.shape[-1]
    row_blocks = tile_data.shape[1]
    slot_count = tile_data.shape[2]
    every_index = jnp.arange(period, dtype=jnp.int32)
    inverse_period = 1.0 / period
    flat_fields = fields.reshape(2, local_phi, flat_width)
    spread = lax.all_to_all(flat_fields, "az", split_axis=2, concat_axis=1, tiled=True)
    cosine_table, sine_table = phase_table(every_index, every_index, period)
    spec_real, spec_imag = forward_mix(
        cosine_table * inverse_period, sine_table * inverse_period, spread[0], spread[1]
    )
    spectrum = lax.all_to_all(
        jnp.stack([spec_real, spec_imag]).astype(jnp.bfloat16),
        "az",
        split_axis=1,
        concat_axis=2,
        tiled=True,
    ).astype(jnp.float32)
    mode_values = spectrum.reshape(2, local_phi, rhs_count, node_count).astype(jnp.bfloat16)
    widened = extended_2(mode_values, (("curve", 3),), block_size)
    extended = widened.reshape(2, local_phi, rhs_count, row_blocks + 2, block_size)
    first_block = lax.axis_index("curve") * row_blocks
    block_total = row_blocks * lax.axis_size("curve")
    relative = jnp.mod(tile_cols - first_block + 1, block_total)
    live_tiles = jnp.arange(slot_count, dtype=jnp.int32)[None, None, :] < tile_count[:, :, None]
    window_index = jnp.arange(row_blocks + 2, dtype=jnp.int32)
    selector = ((relative[..., None] == window_index) & live_tiles[..., None]).astype(jnp.bfloat16)
    picked = jnp.einsum(
        "mbtj,cmrjn->cmrbtn", selector, extended, preferred_element_type=jnp.float32
    ).astype(jnp.bfloat16)
    tile_real = tile_data[:, :, :, 0]
    tile_imag = tile_data[:, :, :, 1]
    near_real = tile_apply(tile_real, picked[0]) - tile_apply(tile_imag, picked[1])
    near_imag = tile_apply(tile_real, picked[1]) + tile_apply(tile_imag, picked[0])
    near_flat = jnp.stack([near_real, near_imag]).reshape(2, local_phi, flat_width)
    collected = lax.all_to_all(near_flat, "az", split_axis=2, concat_axis=1, tiled=True)
    cosine_back, sine_back = phase_table(every_index, every_index, period)
    back_real, back_imag = inverse_mix(cosine_back, sine_back, collected[0], collected[1])
    returned = lax.all_to_all(
        jnp.stack([back_real, back_imag]), "az", split_axis=1, concat_axis=2, tiled=True
    )
    returned = returned.reshape(2, local_phi, rhs_count, node_count)
    imped_real = impedance[0][:, None, :]
    imped_imag = impedance[1][:, None, :]
    out_real = fields[0] + imped_real * returned[0] - imped_imag * returned[1]
    out_imag = fields[1] + imped_real * returned[1] + imped_imag * returned[0]
    return jnp.stack([out_real, out_imag])


def solution(mesh):
    placed = (
        P(None, "az", None, "curve"),
        P(None, "az", "curve"),
        P("az", "curve", None, None, None, None),
        P("az", "curve", None),
        P("az", "curve"),
    )
    return jax.shard_map(
        on_device,
        mesh=mesh,
        in_specs=placed,
        out_specs=P(None, "az", None, "curve"),
        check_vma=False,
    )
```

profile of v0, /device:TPU:57, one launch (start us, length us, event | category | flops | bytes accessed | tf_op | source)
XLA Modules:
  0.0 165.5 jit_solution(17370666663726712444)
XLA Ops:
  0.0 1.8 %copy.60 = f32[2,16,16,128]{1,0,3,2:T(2,128)S(1)} copy(f32[2,16,16,128]{3,2,1,0:T(8,128)} %param.5) | data formatting | bytes 524288 | tf_op args[0]
  1.8 2.9 %reshape.111 = f32[16,1,4096]{2,1,0:T(1,128)S(1)} reshape(f32[2048,2,16]{2,1,0:T(2,128)S(1)} %bitcast.103) | data formatting | bytes 524288
  4.7 41.5 %all_to_all.60 = f32[16,1,4096]{2,1,0:T(1,128)S(1)} all-to-all(f32[16,1,4096]{2,1,0:T(1,128)S(1)} %reshape.111), channel_id=1, replica_groups=mesh['az'=16,'curve'=32] {'az'}, dimensions={0} | all-to-all | bytes 524288 | tf_op jit(solution)/shard_map/all_to_all | solution.py:61
  46.2 0.5 broadcast.113
  46.7 1.2 reduce
  47.9 2.8 %reshape.112 = f32[2048,2,16]{2,1,0:T(2,128)S(1)} reshape(f32[16,4096]{1,0:T(8,128)S(1)} %reduce) | data formatting | bytes 524288
  50.7 0.8 copy.85
  51.5 1.6 fusion.48
  53.2 0.0 copy-start.3
  53.2 0.0 copy-start.4
  53.2 1.6 fusion.46
  54.8 1.3 fusion.36
  56.1 1.3 fusion.35
  57.5 0.8 copy.64
  58.3 4.2 %all-to-all-start.1 = ((bf16[2,256,128]{2,0,1:T(2,128)(2,1)}), bf16[2,256,128]{2,0,1:T(2,128)(2,1)S(1)}, u32[]{:S(2)}, u32[]{:S(2)}) async-start(bf16[2,256,128]{2,0,1:T(2,128)(2,1)} %copy.64), calls=%async_computation.1 | async-start | bytes 262144 | tf_op jit(solution)/shard_map/all_to_all | solution.py:66
  62.5 0.0 copy-done.3
  62.5 0.1 copy.86
  62.6 14.8 %all-to-all-done.1 = bf16[2,256,128]{2,0,1:T(2,128)(2,1)S(1)} async-done(((bf16[2,256,128]{2,0,1:T(2,128)(2,1)}), bf16[2,256,128]{2,0,1:T(2,128)(2,1)S(1)}, u32[]{:S(2)}, u32[]{:S(2)}) %all-to-all-start.1) | async-done | bytes 131104 | tf_op jit(solution)/shard_map/all_to_all | solution.py:66
  77.4 0.1 copy.103
  77.5 1.9 %collective-permute-start = (bf16[2,16,16,128]{3,2,1,0:T(8,128)(2,1)S(1)}, bf16[2,16,16,128]{3,2,1,0:T(8,128)(2,1)S(1)}, u32[]{:S(2)}, u32[]{:S(2)}) collective-permute-start(bf16[2,16,16,128]{3,2,1,0:T(8,128)(2,1)S(1)} %bitcast.109), channel_id=1, source_target_pairs={{0,1},{1,2},{2,3},{3,4},{4,5},{5,6},{6,7},{7,8},{8,9},{9,10},{10,1... | collective-permute-start | bytes 393224 | tf_op jit(solution)/shard_map/ppermute | solution.py:16
  79.4 3.5 %collective-permute-start.1 = (bf16[2,16,16,128]{3,2,1,0:T(8,128)(2,1)S(1)}, bf16[2,16,16,128]{3,2,1,0:T(8,128)(2,1)S(1)}, u32[]{:S(2)}, u32[]{:S(2)}) collective-permute-start(bf16[2,16,16,128]{3,2,1,0:T(8,128)(2,1)S(1)} %bitcast.110), channel_id=1, source_target_pairs={{1,0},{2,1},{3,2},{4,3},{5,4},{6,5},{7,6},{8,7},{9,8},{10,9},{11,1... | collective-permute-start | bytes 393224 | tf_op jit(solution)/shard_map/ppermute | solution.py:17
  83.0 0.0 copy-done.4
  83.0 0.1 iota_compare_fusion.1
  83.0 0.0 copy-start
  83.0 0.7 collective-permute-done
  83.8 4.0 %collective-permute-done.1 = bf16[2,16,16,128]{3,2,1,0:T(8,128)(2,1)S(1)} collective-permute-done((bf16[2,16,16,128]{3,2,1,0:T(8,128)(2,1)S(1)}, bf16[2,16,16,128]{3,2,1,0:T(8,128)(2,1)S(1)}, u32[]{:S(2)}, u32[]{:S(2)}) %collective-permute-start.1) | collective-permute-done | bytes 131104 | tf_op jit(solution)/shard_map/ppermute | solution.py:17
  87.8 0.1 pad_maximum_fusion
  87.8 0.9 reshape.101
  88.8 1.5 fusion.12
  90.3 0.2 slice_bitcast_fusion.1
  90.5 0.0 copy-done
  90.5 0.6 fusion.15
  91.2 1.3 fusion.18
  92.5 0.6 fusion.30
  93.2 0.7 stack.38
  93.8 1.5 fusion.27
  95.4 0.9 pad_maximum_fusion.1
  96.4 1.0 copy.74
  97.4 2.9 %reshape.113 = f32[16,1,4096]{2,1,0:T(1,128)S(1)} reshape(f32[2048,2,16]{2,1,0:T(2,128)S(1)} %bitcast.101) | data formatting | bytes 524288
  100.3 28.4 %all_to_all.61 = f32[16,1,4096]{2,1,0:T(1,128)S(1)} all-to-all(f32[16,1,4096]{2,1,0:T(1,128)S(1)} %reshape.113), channel_id=1, replica_groups=mesh['az'=16,'curve'=32] {'az'}, dimensions={0} | all-to-all | bytes 524288 | tf_op jit(solution)/shard_map/all_to_all | solution.py:90
  128.6 1.2 reduce.1
  129.8 2.8 %reshape.114 = f32[2048,2,16]{2,1,0:T(2,128)S(1)} reshape(f32[16,4096]{1,0:T(8,128)S(1)} %reduce.1) | data formatting | bytes 524288
  132.6 0.8 copy.87
  133.5 1.6 fusion.63
  135.1 1.6 fusion.61
  136.7 0.0 copy-start.2
  136.7 0.0 copy-start.1
  136.7 1.6 fusion.14
  138.3 1.6 fusion.13
  139.9 0.9 copy.78
  140.8 4.3 %all-to-all-start.3 = ((f32[2,256,128]{2,0,1:T(2,128)}), f32[2,256,128]{2,0,1:T(2,128)S(1)}, u32[]{:S(2)}, u32[]{:S(2)}) async-start(f32[2,256,128]{2,0,1:T(2,128)} %copy.78), calls=%async_computation.3 | async-start | bytes 524288 | tf_op jit(solution)/shard_map/all_to_all | solution.py:93
  145.0 0.0 copy-done.2
  145.0 19.6 %all-to-all-done.3 = f32[2,256,128]{2,0,1:T(2,128)S(1)} async-done(((f32[2,256,128]{2,0,1:T(2,128)}), f32[2,256,128]{2,0,1:T(2,128)S(1)}, u32[]{:S(2)}, u32[]{:S(2)}) %all-to-all-start.3) | async-done | bytes 262176 | tf_op jit(solution)/shard_map/all_to_all | solution.py:93
  164.6 0.2 copy.102
  164.8 0.0 copy-done.1
  164.8 0.1 multiply_subtract_fusion
  164.8 0.7 pad_maximum_fusion.3
  (11 shorter events, 0.3 us)
Async XLA Ops:
  53.2 9.3 %copy-start.3 = (s32[16,1,3]{0,1,2:T(1,128)S(1)}, s32[16,1,3]{0,1,2:T(1,128)}, u32[]{:S(2)}) copy-start(s32[16,1,3]{0,1,2:T(1,128)} %param.8) | copy-start | bytes 580
  53.2 29.8 %copy-start.4 = (s32[16,1]{0,1:T(1,128)S(1)}, s32[16,1]{0,1:T(1,128)}, u32[]{:S(2)}) copy-start(s32[16,1]{0,1:T(1,128)} %param.9) | copy-start | bytes 196
  58.3 19.1 %all-to-all-start.1 = ((bf16[2,256,128]{2,0,1:T(2,128)(2,1)}), bf16[2,256,128]{2,0,1:T(2,128)(2,1)S(1)}, u32[]{:S(2)}, u32[]{:S(2)}) async-start(bf16[2,256,128]{2,0,1:T(2,128)(2,1)} %copy.64), calls=%async_computation.1 | async-start | bytes 262144 | tf_op jit(solution)/shard_map/all_to_all | solution.py:66
  77.5 6.3 %collective-permute-start = (bf16[2,16,16,128]{3,2,1,0:T(8,128)(2,1)S(1)}, bf16[2,16,16,128]{3,2,1,0:T(8,128)(2,1)S(1)}, u32[]{:S(2)}, u32[]{:S(2)}) collective-permute-start(bf16[2,16,16,128]{3,2,1,0:T(8,128)(2,1)S(1)} %bitcast.109), channel_id=1, source_target_pairs={{0,1},{1,2},{2,3},{3,4},{4,5},{5,6},{6,7},{7,8},{8,9},{9,10},{10,1... | collective-permute-start | bytes 393224 | tf_op jit(solution)/shard_map/ppermute | solution.py:16
  79.4 8.4 %collective-permute-start.1 = (bf16[2,16,16,128]{3,2,1,0:T(8,128)(2,1)S(1)}, bf16[2,16,16,128]{3,2,1,0:T(8,128)(2,1)S(1)}, u32[]{:S(2)}, u32[]{:S(2)}) collective-permute-start(bf16[2,16,16,128]{3,2,1,0:T(8,128)(2,1)S(1)} %bitcast.110), channel_id=1, source_target_pairs={{1,0},{2,1},{3,2},{4,3},{5,4},{6,5},{7,6},{8,7},{9,8},{10,9},{11,1... | collective-permute-start | bytes 393224 | tf_op jit(solution)/shard_map/ppermute | solution.py:17
  83.0 7.5 %copy-start = (bf16[16,1,3,2,128,128]{5,4,3,2,1,0:T(8,128)(2,1)S(1)}, bf16[16,1,3,2,128,128]{5,4,3,2,1,0:T(8,128)(2,1)}, u32[]{:S(2)}) copy-start(bf16[16,1,3,2,128,128]{5,4,3,2,1,0:T(8,128)(2,1)} %param.7) | copy-start | bytes 9437188
  136.7 8.4 %copy-start.2 = (f32[2,16,128]{2,1,0:T(8,128)S(1)}, f32[2,16,128]{2,1,0:T(8,128)}, u32[]{:S(2)}) copy-start(f32[2,16,128]{2,1,0:T(8,128)} %param.6) | copy-start | bytes 49156
  136.7 28.1 %copy-start.1 = (f32[2,16,16,128]{3,2,1,0:T(8,128)S(1)}, f32[2,16,16,128]{3,2,1,0:T(8,128)}, u32[]{:S(2)}) copy-start(f32[2,16,16,128]{3,2,1,0:T(8,128)} %param.5) | copy-start | bytes 786436
  140.8 23.8 %all-to-all-start.3 = ((f32[2,256,128]{2,0,1:T(2,128)}), f32[2,256,128]{2,0,1:T(2,128)S(1)}, u32[]{:S(2)}, u32[]{:S(2)}) async-start(f32[2,256,128]{2,0,1:T(2,128)} %copy.78), calls=%async_computation.3 | async-start | bytes 524288 | tf_op jit(solution)/shard_map/all_to_all | solution.py:93
where the time goes:
time: 166 us
  blocking collectives  69.8 us (42%)
  waiting for transfers between devices  39.1 us (24%)
  local copies, waits for them, and re-layouts  20.3 us (12%)
  matrix products  17.8 us (11%)
  starting transfers between devices  13.9 us (8%)
  other arithmetic  4.25 us (3%)
    all_to_all x1, blocking collectives, on_device(): lax.all_to_all(flat_fields, 'az', split_axis=2, concat_axis=1, tiled=True)  41.5 us
    all_to_all x1, blocking collectives, on_device(): lax.all_to_all(near_flat, 'az', split_axis=2, concat_axis=1, tiled=True)  28.4 us
    all_to_all x1, waiting for transfers between devices, on_device(): lax.all_to_all(jnp.stack([back_real, back_imag]), 'az', split_axis=1, con...  19.6 us
    all_to_all x1, waiting for transfers between devices, on_device(): lax.all_to_all(jnp.stack([spec_real, spec_imag]).astype(jnp.bfloat16), 'a...  14.8 us
    unnamed x15, local copies, waits for them, and re-layouts  13.2 us
    dot_general x8, matrix products, exact_dot(): jnp.dot(left, right, precision=lax.Precision.HIGHEST, preferred_element_t...  12.1 us
    all_to_all x1, starting transfers between devices, on_device(): lax.all_to_all(jnp.stack([back_real, back_imag]), 'az', split_axis=1, con...  4.26 us
    all_to_all x1, starting transfers between devices, on_device(): lax.all_to_all(jnp.stack([spec_real, spec_imag]).astype(jnp.bfloat16), 'a...  4.22 us
  transfers between devices with their start and end apart: 4, of which 4 were waited for; matrix products, arithmetic and copies ran while one was open for 0% of the time, Pallas kernels for 0%

commit v1 on v0

v1 whole, which is shorter than its diff:
```python
import functools
import math

import jax
import jax.numpy as jnp
import numpy as np
from jax import lax
from jax.experimental import pallas as pl
from jax.experimental.pallas import tpu as pltpu
from jax.sharding import PartitionSpec as P

MESH = pl.DeviceIdType.MESH
F32 = jnp.float32
BF16 = jnp.bfloat16
FIELD_SAME, FIELD_OTHER, MODE_OWN, MODE_OTHER, HALO_UP, HALO_DOWN, NEAR_SAME, NEAR_OTHER, BACK = range(9)
CHUNKS = 2
GROUPS = 8
LOCAL = 16


def transform_tables():
    period = 2 * GROUPS * LOCAL
    half_size = GROUPS * LOCAL
    tables = []
    for half in range(2):
        k = half * half_size + np.arange(half_size).reshape(GROUPS, 1, LOCAL)
        p = np.stack([side * half_size + np.arange(half_size) for side in (half, 1 - half)])
        p = p.reshape(2, GROUPS, 1, LOCAL)
        product = (k.reshape(-1, 1) * p.reshape(1, -1)) % period
        angle = 2.0 * math.pi / period * product
        cosine = np.cos(angle).reshape(GROUPS, LOCAL, 2, GROUPS, LOCAL)
        sine = np.sin(angle).reshape(GROUPS, LOCAL, 2, GROUPS, LOCAL)
        full = np.zeros((GROUPS, 2, LOCAL, 2, GROUPS, 2, LOCAL))
        full[:, 0, :, :, :, 0, :] = cosine
        full[:, 0, :, :, :, 1, :] = sine
        full[:, 1, :, :, :, 0, :] = -sine
        full[:, 1, :, :, :, 1, :] = cosine
        full = full.reshape(2 * half_size, 4 * half_size)
        high = full.astype(np.float32).astype(jnp.bfloat16)
        low = (full - high.astype(np.float64)).astype(np.float32).astype(jnp.bfloat16)
        tables.append(np.stack([high, low]))
    return np.stack(tables)


def dot(left, right):
    return jnp.dot(left, right, preferred_element_type=F32)


def split(value):
    high = value.astype(BF16)
    low = (value - high.astype(F32)).astype(BF16)
    return high, low


def kernel(
    fields_ref,
    imped_ref,
    cols_ref,
    count_ref,
    tiles_hbm,
    tables_hbm,
    out_ref,
    tiles,
    tables,
    stage,
    field_same,
    field_other,
    modes,
    window,
    spread,
    near,
    near_stage,
    near_same,
    near_other,
    back,
    returned,
    send_sem,
    recv_sem,
    load_sem,
):
    az = lax.axis_index("az")
    curve = lax.axis_index("curve")
    blocks = lax.axis_size("curve")
    half = az // GROUPS
    me = az % GROUPS
    base = half * GROUPS
    far = (1 - half) * GROUPS
    last = blocks - 1
    at_end = jnp.logical_or(curve == 0, curve == last)
    across = (az + GROUPS) % (2 * GROUPS)
    up = (jnp.where(curve == last, across, az), (curve + 1) % blocks)
    down = (jnp.where(curve == 0, across, az), (curve + last) % blocks)
    up_source = jnp.where(curve == last, 3, 1)
    down_source = jnp.where(curve == 0, 3, 1)

    def peer(step):
        return (me + step) % GROUPS

    barrier = pltpu.get_barrier_semaphore()
    for step in range(GROUPS):
        pl.semaphore_signal(barrier, inc=1, device_id=(far + peer(step), curve), device_id_type=MESH)
    for device in (up, down):
        pl.semaphore_signal(barrier, inc=1, device_id=device, device_id_type=MESH)
    for step in range(1, GROUPS):
        pl.semaphore_signal(barrier, inc=1, device_id=(base + peer(step), curve), device_id_type=MESH)

    table_load = pltpu.make_async_copy(tables_hbm, tables, load_sem.at[0])
    table_load.start()
    tile_load = pltpu.make_async_copy(tiles_hbm, tiles, load_sem.at[1])
    tile_load.start()

    def remote(source, target, row, chunk, device):
        pltpu.make_async_remote_copy(
            src_ref=source,
            dst_ref=target,
            send_sem=send_sem.at[row, chunk],
            recv_sem=recv_sem.at[row, chunk],
            device_id=device,
            device_id_type=MESH,
        ).start()

    def take(ref, row, chunk):
        pltpu.make_async_copy(ref, ref, recv_sem.at[row, chunk]).wait()

    def drain(ref, row, chunk):
        pltpu.make_async_copy(ref, ref, send_sem.at[row, chunk]).wait()

    def exchange(source, same, other, same_row, other_row, chunk):
        for step in range(GROUPS):
            group = peer(step)
            remote(source.at[chunk, group, 0], other.at[chunk, me], other_row, chunk, (far + group, curve))
        for step in range(1, GROUPS):
            group = peer(step)
            remote(source.at[chunk, group], same.at[chunk, :, me], same_row, chunk, (base + group, curve))
        same[chunk, 0, me] = source[chunk, me, 0]
        same[chunk, 1, me] = source[chunk, me, 1]

    def rows_of(value):
        return value.reshape(GROUPS * 2 * LOCAL, value.shape[-1])

    width = GROUPS * 2 * LOCAL

    def transform_same(same, chunk, side, first):
        columns = pl.ds(first * width, width)
        high = rows_of(same[chunk, 0])
        low = rows_of(same[chunk, 1])
        return (
            dot(tables[side, 0, :, columns], high)
            + dot(tables[side, 0, :, columns], low)
            + dot(tables[side, 1, :, columns], high)
        )

    def transform_other(other, chunk, side, first):
        columns = pl.ds(first * width, width)
        high = rows_of(other[chunk])
        return dot(tables[side, 0, :, columns], high) + dot(tables[side, 1, :, columns], high)

    for chunk in range(CHUNKS):
        for group in range(GROUPS):
            rows = fields_ref[pl.ds(group + GROUPS * chunk, 2 * LOCAL, stride=CHUNKS * GROUPS), :]
            high, low = split(rows)
            stage[chunk, group, 0] = high
            stage[chunk, group, 1] = low

    pl.semaphore_wait(barrier, 2 * GROUPS + 1)
    for chunk in range(CHUNKS):
        exchange(stage, field_same, field_other, FIELD_SAME, FIELD_OTHER, chunk)
    table_load.wait()

    def forward(chunk):
        take(field_same.at[chunk, :, pl.ds(0, GROUPS - 1)], FIELD_SAME, chunk)
        total = transform_same(field_same, chunk, half, 0)
        take(field_other.at[chunk], FIELD_OTHER, chunk)
        total = total + transform_other(field_other, chunk, half, 1)
        scale = 1.0 / (2 * GROUPS * LOCAL)
        modes[chunk, 0] = (total * scale).astype(BF16).reshape(modes.shape[2:])
        for step in range(1, GROUPS):
            group = peer(step)
            remote(modes.at[chunk, 0, group], window.at[chunk, 1, me], MODE_OWN, chunk, (base + group, curve))
        window[chunk, 1, me] = modes[chunk, 0, me]

        @pl.when(at_end)
        def _():
            wrapped = transform_same(field_same, chunk, 1 - half, 1)
            wrapped = wrapped + transform_other(field_other, chunk, 1 - half, 0)
            modes[chunk, 1] = (wrapped * scale).astype(BF16).reshape(modes.shape[2:])
            for step in range(1, GROUPS):
                group = peer(step)
                remote(modes.at[chunk, 1, group], window.at[chunk, 3, me], MODE_OTHER, chunk, (base + group, curve))
            window[chunk, 3, me] = modes[chunk, 1, me]

    def halo(chunk):
        take(window.at[chunk, 1, pl.ds(0, GROUPS - 1)], MODE_OWN, chunk)

        @pl.when(at_end)
        def _():
            take(window.at[chunk, 3, pl.ds(0, GROUPS - 1)], MODE_OTHER, chunk)

        remote(window.at[chunk, up_source], window.at[chunk, 0], HALO_UP, chunk, up)
        remote(window.at[chunk, down_source], window.at[chunk, 2], HALO_DOWN, chunk, down)

    def slot_of(mode, place):
        block = (curve + place + last) % blocks
        slot = jnp.where(cols_ref[mode, 0] == block, 0, jnp.where(cols_ref[mode, 1] == block, 1, 2))
        return slot, jnp.where(slot < count_ref[mode], 1.0, 0.0).astype(F32)

    def product(mode, place):
        slot, weight = slot_of(mode, place)
        real = spread[place, pl.ds(mode, GROUPS, stride=2 * LOCAL), :] * weight
        imag = spread[place, pl.ds(mode + LOCAL, GROUPS, stride=2 * LOCAL), :] * -weight
        left = jnp.concatenate([real, imag], axis=0)
        right = jnp.concatenate([imag, -real], axis=0)
        both = jnp.concatenate([left, right], axis=1).astype(BF16)
        tile = jnp.concatenate([tiles[mode, slot, 0], tiles[mode, slot, 1]], axis=1)
        return lax.dot_general(both, tile, (((1,), (1,)), ((), ())), preferred_element_type=F32)

    unroll = 4

    def near_own(chunk):
        spread[1] = rows_of(window[chunk, 1]).astype(F32)

        def body(index, carry):
            for inner in range(unroll):
                mode = index * unroll + inner
                total = product(mode, 1)
                near[chunk, pl.ds(mode, GROUPS, stride=2 * LOCAL), :] = total[:GROUPS]
                near[chunk, pl.ds(mode + LOCAL, GROUPS, stride=2 * LOCAL), :] = total[GROUPS:]
            return carry

        lax.fori_loop(0, LOCAL // unroll, body, 0)

    def near_rest(chunk):
        take(window.at[chunk, 0], HALO_UP, chunk)
        take(window.at[chunk, 2], HALO_DOWN, chunk)
        spread[0] = rows_of(window[chunk, 0]).astype(F32)
        spread[2] = rows_of(window[chunk, 2]).astype(F32)

        def body(index, carry):
            for inner in range(unroll):
                mode = index * unroll + inner
                total = product(mode, 0) + product(mode, 2)
                real = pl.ds(mode, GROUPS, stride=2 * LOCAL)
                imag = pl.ds(mode + LOCAL, GROUPS, stride=2 * LOCAL)
                near[chunk, real, :] = near[chunk, real, :] + total[:GROUPS]
                near[chunk, imag, :] = near[chunk, imag, :] + total[GROUPS:]
            return carry

        lax.fori_loop(0, LOCAL // unroll, body, 0)
        high, low = split(near[chunk])
        near_stage[chunk, :, 0] = high.reshape(GROUPS, 2 * LOCAL, high.shape[-1])
        near_stage[chunk, :, 1] = low.reshape(GROUPS, 2 * LOCAL, low.shape[-1])
        exchange(near_stage, near_same, near_other, NEAR_SAME, NEAR_OTHER, chunk)

    def inverse(chunk):
        take(near_same.at[chunk, :, pl.ds(0, GROUPS - 1)], NEAR_SAME, chunk)
        total = transform_same(near_same, chunk, half, 0)
        take(near_other.at[chunk], NEAR_OTHER, chunk)
        total = total + transform_other(near_other, chunk, half, 1)
        back[chunk] = total.reshape(back.shape[1:])
        for step in range(1, GROUPS):
            group = peer(step)
            target = returned.at[chunk, pl.ds(pl.multiple_of(me * 2 * LOCAL, 2 * LOCAL), 2 * LOCAL)]
            remote(back.at[chunk, group], target, BACK, chunk, (base + group, curve))
        returned[chunk, pl.ds(pl.multiple_of(me * 2 * LOCAL, 2 * LOCAL), 2 * LOCAL)] = back[chunk, me]

    def combine(chunk):
        take(returned.at[chunk, pl.ds(0, (GROUPS - 1) * 2 * LOCAL)], BACK, chunk)
        for point in range(LOCAL):
            real = returned[chunk, pl.ds(point, GROUPS, stride=2 * LOCAL), :]
            minus_imag = returned[chunk, pl.ds(point + LOCAL, GROUPS, stride=2 * LOCAL), :]
            imped_real = imped_ref[pl.ds(point, 1), :]
            imped_imag = imped_ref[pl.ds(point + LOCAL, 1), :]
            row = point * CHUNKS * GROUPS + chunk * GROUPS
            rows = pl.ds(row, GROUPS)
            out_ref[rows, :] = fields_ref[rows, :] + imped_real * real + imped_imag * minus_imag
            rows = pl.ds(row + LOCAL * CHUNKS * GROUPS, GROUPS)
            out_ref[rows, :] = fields_ref[rows, :] - imped_real * minus_imag + imped_imag * real

    forward(0)
    halo(0)
    forward(1)
    tile_load.wait()
    near_own(0)
    halo(1)
    near_rest(0)
    near_own(1)
    near_rest(1)
    inverse(0)
    inverse(1)
    combine(0)
    combine(1)

    for chunk in range(CHUNKS):
        drain(field_same.at[chunk, :, pl.ds(0, GROUPS - 1)], FIELD_SAME, chunk)
        drain(field_other.at[chunk], FIELD_OTHER, chunk)
        drain(window.at[chunk, 1, pl.ds(0, GROUPS - 1)], MODE_OWN, chunk)

        @pl.when(at_end)
        def _():
            drain(window.at[chunk, 3, pl.ds(0, GROUPS - 1)], MODE_OTHER, chunk)

        drain(window.at[chunk, 0], HALO_UP, chunk)
        drain(window.at[chunk, 2], HALO_DOWN, chunk)
        drain(near_same.at[chunk, :, pl.ds(0, GROUPS - 1)], NEAR_SAME, chunk)
        drain(near_other.at[chunk], NEAR_OTHER, chunk)
        drain(returned.at[chunk, pl.ds(0, (GROUPS - 1) * 2 * LOCAL)], BACK, chunk)


def on_device(tables, fields, impedance, tile_data, tile_cols, tile_count):
    points, rhs, nodes = fields.shape[1:]
    block = tile_data.shape[-1]
    modes, _, slots = tile_data.shape[:3]
    pair = 2 * LOCAL
    whole = GROUPS * pair
    vmem = pl.BlockSpec(memory_space=pltpu.VMEM)
    smem = pl.BlockSpec(memory_space=pltpu.SMEM)
    hbm = pl.BlockSpec(memory_space=pl.ANY)
    out = pl.pallas_call(
        kernel,
        out_shape=jax.ShapeDtypeStruct((2 * points * rhs, nodes), F32),
        in_specs=[vmem, vmem, smem, smem, hbm, hbm],
        out_specs=vmem,
        scratch_shapes=[
            pltpu.VMEM((modes, slots, 2, block, block), BF16),
            pltpu.VMEM(tables.shape, BF16),
            pltpu.VMEM((CHUNKS, GROUPS, 2, pair, nodes), BF16),
            pltpu.VMEM((CHUNKS, 2, GROUPS, pair, nodes), BF16),
            pltpu.VMEM((CHUNKS, GROUPS, pair, nodes), BF16),
            pltpu.VMEM((CHUNKS, 2, GROUPS, pair, nodes), BF16),
            pltpu.VMEM((CHUNKS, 4, GROUPS, pair, nodes), BF16),
            pltpu.VMEM((3, whole, nodes), F32),
            pltpu.VMEM((CHUNKS, whole, nodes), F32),
            pltpu.VMEM((CHUNKS, GROUPS, 2, pair, nodes), BF16),
            pltpu.VMEM((CHUNKS, 2, GROUPS, pair, nodes), BF16),
            pltpu.VMEM((CHUNKS, GROUPS, pair, nodes), BF16),
            pltpu.VMEM((CHUNKS, GROUPS, pair, nodes), F32),
            pltpu.VMEM((CHUNKS, whole, nodes), F32),
            pltpu.SemaphoreType.DMA((9, CHUNKS)),
            pltpu.SemaphoreType.DMA((9, CHUNKS)),
            pltpu.SemaphoreType.DMA((2,)),
        ],
        compiler_params=pltpu.CompilerParams(collective_id=0, has_side_effects=True),
    )(
        fields.reshape(2 * points * rhs, nodes),
        impedance.reshape(2 * points, nodes),
        tile_cols.reshape(modes, slots),
        tile_count.reshape(modes),
        tile_data.reshape(modes, slots, 2, block, block),
        tables,
    )
    return out.reshape(fields.shape)


def solution(mesh):
    placed = (
        P(None, "az", None, "curve"),
        P(None, "az", "curve"),
        P("az", "curve", None, None, None, None),
        P("az", "curve", None),
        P("az", "curve"),
    )

    def apply(*arrays):
        tables = jnp.asarray(transform_tables())
        return jax.shard_map(
            on_device,
            mesh=mesh,
            in_specs=(P(),) + placed,
            out_specs=P(None, "az", None, "curve"),
            check_vma=False,
        )(tables, *arrays)

    return apply
```

time: 166 us -> 72.1 us (0.43)
  the two profiles are of different devices: /device:TPU:57 before, /device:TPU:65 now
where the time goes in v1:
time: 72.1 us; the launch traced here: 71.9 us
  Pallas kernels  68.9 us (96%)
  local copies, waits for them, and re-layouts  3.02 us (4%)
    pallas_call x1, Pallas kernels, on_device(): pl.pallas_call(kernel, out_shape=jax.ShapeDtypeStruct((2 * points * rhs,...  68.9 us
    unnamed x1, local copies, waits for them, and re-layouts  1.67 us

profile of v1, /device:TPU:65, one launch (start us, length us, event | category | flops | bytes accessed | tf_op | source)
XLA Modules:
  0.0 71.9 jit_solution(17589131389631740542)
XLA Ops:
  0.0 1.4 %copy.8 = s32[16,1,3]{2,0,1:T(8,128)} copy(s32[16,1,3]{0,1,2:T(1,128)} %param.9) | data formatting | bytes 384 | tf_op jit(solution)/shard_map/reshape | solution.py:346
  1.4 68.9 %shard_map.64 = f32[512,128]{1,0:T(8,128)} custom-call(f32[512,128]{1,0:T(8,128)} %bitcast.8, f32[32,128]{1,0:T(8,128)} %bitcast.10, s32[16,3]{1,0:T(8,128)} %bitcast.9, s32[16]{0:T(128)} %bitcast.11, bf16[16,3,2,128,128]{4,3,2,1,0:T(8,128)(2,1)} %bitcast.6, bf16[2,2,256,512]{3,2,1,0:T(8,128)(2,1)} %constant.2.clone.tables_hbm), custom_call_target="tpu_custom_call" | custom-call | tf_op jit(solution)/shard_map/pallas_call | solution.py:318
  70.2 1.7 %copy.10 = f32[2,16,16,128]{3,2,1,0:T(8,128)} copy(f32[2,16,16,128]{3,2,1,0:T(8,128)} %bitcast.7) | data formatting | bytes 524288

commit v2 on v1

v2 whole, which is shorter than its diff:
```python
import functools
import math

import jax
import jax.numpy as jnp
import numpy as np
from jax import lax
from jax.experimental import pallas as pl
from jax.experimental.pallas import tpu as pltpu
from jax.sharding import PartitionSpec as P

MESH = pl.DeviceIdType.MESH
F32 = jnp.float32
BF16 = jnp.bfloat16
FIELD, FIELD_OTHER, MODE_OWN, MODE_OTHER, PART, FAR_PART, WRAP_PART, WRAP_FAR = range(8)
HALO_UP, HALO_DOWN, NEAR_SAME, NEAR_OTHER, BACK, BACK_FAR = range(8, 14)
CHUNKS = 2
GROUPS = 8
LOCAL = 16


def transform_tables():
    period = 2 * GROUPS * LOCAL
    half_size = GROUPS * LOCAL
    tables = []
    for half in range(2):
        k = half * half_size + np.arange(half_size).reshape(GROUPS, 1, LOCAL)
        p = np.stack([side * half_size + np.arange(half_size) for side in (half, 1 - half)])
        p = p.reshape(2, GROUPS, 1, LOCAL)
        product = (k.reshape(-1, 1) * p.reshape(1, -1)) % period
        angle = 2.0 * math.pi / period * product
        cosine = np.cos(angle).reshape(GROUPS, LOCAL, 2, GROUPS, LOCAL)
        sine = np.sin(angle).reshape(GROUPS, LOCAL, 2, GROUPS, LOCAL)
        full = np.zeros((GROUPS, 2, LOCAL, 2, GROUPS, 2, LOCAL))
        full[:, 0, :, :, :, 0, :] = cosine
        full[:, 0, :, :, :, 1, :] = sine
        full[:, 1, :, :, :, 0, :] = -sine
        full[:, 1, :, :, :, 1, :] = cosine
        full = full.reshape(2 * half_size, 4 * half_size)
        high = full.astype(np.float32).astype(jnp.bfloat16)
        low = (full - high.astype(np.float64)).astype(np.float32).astype(jnp.bfloat16)
        tables.append(np.stack([high, low]))
    return np.stack(tables)


def dot(left, right):
    return jnp.dot(left, right, preferred_element_type=F32)


def split(value):
    high = value.astype(BF16)
    low = (value - high.astype(F32)).astype(BF16)
    return high, low


def kernel(
    fields_hbm,
    imped_ref,
    cols_ref,
    count_ref,
    tiles_hbm,
    tables_hbm,
    out,
    fields,
    tiles,
    turned,
    tables,
    stage,
    field_same,
    field_other,
    modes,
    part,
    far_part,
    part_in,
    far_in,
    window,
    spread,
    near,
    near_stage,
    near_same,
    near_other,
    back,
    returned,
    back_far,
    returned_far,
    send_sem,
    recv_sem,
    load_sem,
):
    az = lax.axis_index("az")
    curve = lax.axis_index("curve")
    blocks = lax.axis_size("curve")
    half = az // GROUPS
    me = az % GROUPS
    base = half * GROUPS
    far = (1 - half) * GROUPS
    last = blocks - 1
    at_end = jnp.logical_or(curve == 0, curve == last)
    across = (az + GROUPS) % (2 * GROUPS)
    up = (jnp.where(curve == last, across, az), (curve + 1) % blocks)
    down = (jnp.where(curve == 0, across, az), (curve + last) % blocks)
    up_source = jnp.where(curve == last, 3, 1)
    down_source = jnp.where(curve == 0, 3, 1)

    def peer(step):
        return (me + step) % GROUPS

    barrier = pltpu.get_barrier_semaphore()
    greeted = [(far + peer(step), curve) for step in range(GROUPS)]
    greeted += [up, down] + [(base + peer(step), curve) for step in range(1, GROUPS)]
    for device in greeted:
        pl.semaphore_signal(barrier, inc=1, device_id=device, device_id_type=MESH)

    def field_load(chunk):
        rows = pl.ds(chunk * GROUPS, GROUPS)
        return pltpu.make_async_copy(fields_hbm.at[:, rows], fields.at[chunk], load_sem.at[5 + chunk])

    for chunk in range(CHUNKS):
        field_load(chunk).start()
    table_load = pltpu.make_async_copy(tables_hbm, tables, load_sem.at[1])
    table_load.start()
    tile_load = pltpu.make_async_copy(tiles_hbm, tiles, load_sem.at[2])
    tile_load.start()

    def remote(source, target, row, chunk, device):
        pltpu.make_async_remote_copy(
            src_ref=source,
            dst_ref=target,
            send_sem=send_sem.at[row, chunk],
            recv_sem=recv_sem.at[row, chunk],
            device_id=device,
            device_id_type=MESH,
        ).start()

    def take(ref, row, chunk):
        pltpu.make_async_copy(ref, ref, recv_sem.at[row, chunk]).wait()

    def drain(ref, row, chunk):
        pltpu.make_async_copy(ref, ref, send_sem.at[row, chunk]).wait()

    def send_same(source, same, row, chunk):
        for step in range(1, GROUPS):
            group = peer(step)
            remote(source.at[chunk, group], same.at[chunk, :, me], row, chunk, (base + group, curve))
        same[chunk, 0, me] = source[chunk, me, 0]
        same[chunk, 1, me] = source[chunk, me, 1]

    def send_other(source, other, row, chunk):
        for step in range(GROUPS):
            group = peer(step)
            remote(source.at[chunk, group, 0], other.at[me], row, chunk, (far + group, curve))

    def rows_of(value):
        return value.reshape(GROUPS * 2 * LOCAL, value.shape[-1])

    width = GROUPS * 2 * LOCAL

    def transform_same(same, chunk, side, first):
        columns = pl.ds(first * width, width)
        high = rows_of(same[chunk, 0])
        low = rows_of(same[chunk, 1])
        return (
            dot(tables[side, 0, :, columns], high)
            + dot(tables[side, 0, :, columns], low)
            + dot(tables[side, 1, :, columns], high)
        )

    def transform_other(other, side, first):
        columns = pl.ds(first * width, width)
        high = rows_of(other[...])
        return dot(tables[side, 0, :, columns], high) + dot(tables[side, 1, :, columns], high)

    def fill(chunk):
        field_load(chunk).wait()
        for group in range(GROUPS):
            high, low = split(fields[chunk, :, group, :])
            stage[chunk, group, 0] = high
            stage[chunk, group, 1] = low

    fill(0)
    fill(1)
    pl.semaphore_wait(barrier, len(greeted))
    send_other(stage, field_other, FIELD_OTHER, 0)
    send_same(stage, field_same, FIELD, 1)
    send_same(stage, field_same, FIELD, 0)
    table_load.wait()

    def send_far(kind, row, chunk):
        for step in range(GROUPS):
            group = peer(step)
            remote(far_part.at[chunk, kind, group], far_in.at[chunk, kind, me], row, chunk, (far + group, curve))

    def send_near(kind, row, chunk):
        for step in range(1, GROUPS):
            group = peer(step)
            remote(part.at[chunk, kind, group], part_in.at[chunk, kind, me], row, chunk, (base + group, curve))
        part_in[chunk, kind, me] = part[chunk, kind, me]

    scale = 1.0 / (2 * GROUPS * LOCAL)

    def send_modes(total, kind, place, row, chunk):
        modes[kind] = (total * scale).astype(BF16).reshape(modes.shape[1:])
        for step in range(1, GROUPS):
            group = peer(step)
            remote(modes.at[kind, group], window.at[chunk, place, me], row, chunk, (base + group, curve))
        window[chunk, place, me] = modes[kind, me]

    def forward_first(chunk):
        take(field_same.at[chunk, :, pl.ds(0, GROUPS - 1)], FIELD, chunk)
        total = transform_same(field_same, chunk, half, 0)
        take(field_other, FIELD_OTHER, chunk)
        send_modes(total + transform_other(field_other, half, 1), 0, 1, MODE_OWN, chunk)

        @pl.when(at_end)
        def _():
            wrapped = transform_same(field_same, chunk, 1 - half, 1) + transform_other(field_other, 1 - half, 0)
            send_modes(wrapped, 1, 3, MODE_OTHER, chunk)

    def forward_last(chunk):
        take(field_same.at[chunk, :, pl.ds(0, GROUPS - 1)], FIELD, chunk)
        theirs = transform_same(field_same, chunk, 1 - half, 1)
        far_part[chunk, 0] = theirs.astype(BF16).reshape(far_part.shape[2:])
        send_far(0, FAR_PART, chunk)
        ours = transform_same(field_same, chunk, half, 0)
        part[chunk, 0] = ours.reshape(part.shape[2:])
        send_near(0, PART, chunk)

        @pl.when(at_end)
        def _():
            far_part[chunk, 1] = part[chunk, 0].astype(BF16)
            send_far(1, WRAP_FAR, chunk)
            part[chunk, 1] = theirs.reshape(part.shape[2:])
            send_near(1, WRAP_PART, chunk)

    def settle(chunk, kind, place):
        total = part_in[chunk, kind] + far_in[chunk, kind].astype(F32)
        window[chunk, place] = (total * scale).astype(BF16)

    def halo(chunk):
        if chunk == 0:
            take(window.at[chunk, 1, pl.ds(0, GROUPS - 1)], MODE_OWN, chunk)

            @pl.when(at_end)
            def _():
                take(window.at[chunk, 3, pl.ds(0, GROUPS - 1)], MODE_OTHER, chunk)
        else:
            take(part_in.at[chunk, 0, pl.ds(0, GROUPS - 1)], PART, chunk)
            take(far_in.at[chunk, 0], FAR_PART, chunk)
            settle(chunk, 0, 1)

            @pl.when(at_end)
            def _():
                take(part_in.at[chunk, 1, pl.ds(0, GROUPS - 1)], WRAP_PART, chunk)
                take(far_in.at[chunk, 1], WRAP_FAR, chunk)
                settle(chunk, 1, 3)

        remote(window.at[chunk, up_source], window.at[chunk, 0], HALO_UP, chunk, up)
        remote(window.at[chunk, down_source], window.at[chunk, 2], HALO_DOWN, chunk, down)

    def slot_of(mode, place):
        block = (curve + place + last) % blocks
        slot = jnp.where(cols_ref[0, 0, mode] == block, 0, jnp.where(cols_ref[1, 0, mode] == block, 1, 2))
        return slot, jnp.where(slot < count_ref[mode], 1.0, 0.0).astype(F32)

    def prepare():
        def body(mode, carry):
            for index, place in enumerate((1, 0, 2)):
                slot, weight = slot_of(mode, place)
                for kind in range(2):
                    tile = tiles[mode, slot, kind].astype(F32) * weight
                    turned[mode, index, kind] = jnp.transpose(tile).astype(BF16)
            return carry

        lax.fori_loop(0, LOCAL, body, 0)

    def spectrum_rows(mode, place):
        real = spread[place, pl.ds(mode, GROUPS, stride=2 * LOCAL), :]
        minus_imag = -spread[place, pl.ds(mode + LOCAL, GROUPS, stride=2 * LOCAL), :]
        left = jnp.concatenate([real, minus_imag], axis=0)
        right = jnp.concatenate([minus_imag, -real], axis=0)
        return [left.astype(BF16), right.astype(BF16)]

    def product(mode, places, first):
        left = jnp.concatenate([part for place in places for part in spectrum_rows(mode, place)], axis=1)
        right = turned[mode, pl.ds(first, len(places))]
        return dot(left, right.reshape(left.shape[1], right.shape[-1]))

    unroll = 4

    def near_own(chunk):
        spread[1] = rows_of(window[chunk, 1]).astype(F32)

        def body(index, carry):
            for inner in range(unroll):
                mode = index * unroll + inner
                total = product(mode, (1,), 0)
                near[chunk, pl.ds(mode, GROUPS, stride=2 * LOCAL), :] = total[:GROUPS]
                near[chunk, pl.ds(mode + LOCAL, GROUPS, stride=2 * LOCAL), :] = total[GROUPS:]
            return carry

        lax.fori_loop(0, LOCAL // unroll, body, 0)

    def near_rest(chunk):
        take(window.at[chunk, 0], HALO_UP, chunk)
        take(window.at[chunk, 2], HALO_DOWN, chunk)
        spread[0] = rows_of(window[chunk, 0]).astype(F32)
        spread[2] = rows_of(window[chunk, 2]).astype(F32)

        def body(index, carry):
            for inner in range(unroll):
                mode = index * unroll + inner
                total = product(mode, (0, 2), 1)
                real = pl.ds(mode, GROUPS, stride=2 * LOCAL)
                imag = pl.ds(mode + LOCAL, GROUPS, stride=2 * LOCAL)
                near[chunk, real, :] = near[chunk, real, :] + total[:GROUPS]
                near[chunk, imag, :] = near[chunk, imag, :] + total[GROUPS:]
            return carry

        lax.fori_loop(0, LOCAL // unroll, body, 0)
        high, low = split(near[chunk])
        near_stage[chunk, :, 0] = high.reshape(GROUPS, 2 * LOCAL, high.shape[-1])
        near_stage[chunk, :, 1] = low.reshape(GROUPS, 2 * LOCAL, low.shape[-1])
        if chunk == 0:
            send_other(near_stage, near_other, NEAR_OTHER, chunk)
            send_same(near_stage, near_same, NEAR_SAME, chunk)
        else:
            send_same(near_stage, near_same, NEAR_SAME, chunk)

    mine = pl.ds(pl.multiple_of(me * 2 * LOCAL, 2 * LOCAL), 2 * LOCAL)

    def send_back(total, chunk):
        back[chunk] = total.reshape(back.shape[1:])
        for step in range(1, GROUPS):
            group = peer(step)
            remote(back.at[chunk, group], returned.at[chunk, mine], BACK, chunk, (base + group, curve))
        returned[chunk, mine] = back[chunk, me]

    def inverse_first(chunk):
        take(near_same.at[chunk, :, pl.ds(0, GROUPS - 1)], NEAR_SAME, chunk)
        total = transform_same(near_same, chunk, half, 0)
        take(near_other, NEAR_OTHER, chunk)
        send_back(total + transform_other(near_other, half, 1), chunk)

    def inverse_last(chunk):
        take(near_same.at[chunk, :, pl.ds(0, GROUPS - 1)], NEAR_SAME, chunk)
        theirs = transform_same(near_same, chunk, 1 - half, 1)
        back_far[...] = theirs.astype(BF16).reshape(back_far.shape)
        for step in range(GROUPS):
            group = peer(step)
            remote(back_far.at[group], returned_far.at[me], BACK_FAR, chunk, (far + group, curve))
        send_back(transform_same(near_same, chunk, half, 0), chunk)

    def combine(chunk):
        take(returned.at[chunk, pl.ds(0, (GROUPS - 1) * 2 * LOCAL)], BACK, chunk)
        if chunk > 0:
            take(returned_far, BACK_FAR, chunk)
            returned[chunk] = returned[chunk] + rows_of(returned_far[...]).astype(F32)
        for point in range(LOCAL):
            real = returned[chunk, pl.ds(point, GROUPS, stride=2 * LOCAL), :]
            minus_imag = returned[chunk, pl.ds(point + LOCAL, GROUPS, stride=2 * LOCAL), :]
            imped_real = imped_ref[pl.ds(point, 1), :]
            imped_imag = imped_ref[pl.ds(point + LOCAL, 1), :]
            rows = pl.ds(chunk * GROUPS, GROUPS)
            out[point, rows, :] = imped_real * real + imped_imag * minus_imag
            out[point + LOCAL, rows, :] = imped_imag * real - imped_real * minus_imag

    forward_last(1)
    tile_load.wait()
    prepare()
    forward_first(0)
    halo(0)
    halo(1)
    near_own(0)
    near_own(1)
    near_rest(0)
    near_rest(1)
    inverse_last(1)
    inverse_first(0)
    combine(0)
    combine(1)

    drain(field_other, FIELD_OTHER, 0)
    drain(window.at[0, 1, pl.ds(0, GROUPS - 1)], MODE_OWN, 0)
    drain(far_in.at[1, 0], FAR_PART, 1)
    drain(part_in.at[1, 0, pl.ds(0, GROUPS - 1)], PART, 1)

    @pl.when(at_end)
    def _():
        drain(window.at[0, 3, pl.ds(0, GROUPS - 1)], MODE_OTHER, 0)
        drain(far_in.at[1, 1], WRAP_FAR, 1)
        drain(part_in.at[1, 1, pl.ds(0, GROUPS - 1)], WRAP_PART, 1)

    for chunk in range(CHUNKS):
        drain(field_same.at[chunk, :, pl.ds(0, GROUPS - 1)], FIELD, chunk)
        drain(window.at[chunk, 0], HALO_UP, chunk)
        drain(window.at[chunk, 2], HALO_DOWN, chunk)
        drain(near_same.at[chunk, :, pl.ds(0, GROUPS - 1)], NEAR_SAME, chunk)
        if chunk == 0:
            drain(near_other, NEAR_OTHER, chunk)
        else:
            drain(returned_far, BACK_FAR, chunk)
        drain(returned.at[chunk, pl.ds(0, (GROUPS - 1) * 2 * LOCAL)], BACK, chunk)


def on_device(tables, fields, impedance, tile_data, tile_cols, tile_count):
    points, rhs, nodes = fields.shape[1:]
    block = tile_data.shape[-1]
    modes, _, slots = tile_data.shape[:3]
    pair = 2 * LOCAL
    whole = GROUPS * pair
    vmem = pl.BlockSpec(memory_space=pltpu.VMEM)
    smem = pl.BlockSpec(memory_space=pltpu.SMEM)
    hbm = pl.BlockSpec(memory_space=pl.ANY)
    out = pl.pallas_call(
        kernel,
        out_shape=pltpu.VMEM((2 * points, rhs, nodes), F32),
        in_specs=[hbm, vmem, smem, smem, hbm, hbm],
        out_specs=vmem,
        scratch_shapes=[
            pltpu.VMEM((CHUNKS, 2 * points, GROUPS, nodes), F32),
            pltpu.VMEM((modes, slots, 2, block, block), BF16),
            pltpu.VMEM((modes, slots, 2, block, block), BF16),
            pltpu.VMEM(tables.shape, BF16),
            pltpu.VMEM((CHUNKS, GROUPS, 2, pair, nodes), BF16),
            pltpu.VMEM((CHUNKS, 2, GROUPS, pair, nodes), BF16),
            pltpu.VMEM((GROUPS, pair, nodes), BF16),
            pltpu.VMEM((2, GROUPS, pair, nodes), BF16),
            pltpu.VMEM((CHUNKS, 2, GROUPS, pair, nodes), F32),
            pltpu.VMEM((CHUNKS, 2, GROUPS, pair, nodes), BF16),
            pltpu.VMEM((CHUNKS, 2, GROUPS, pair, nodes), F32),
            pltpu.VMEM((CHUNKS, 2, GROUPS, pair, nodes), BF16),
            pltpu.VMEM((CHUNKS, 4, GROUPS, pair, nodes), BF16),
            pltpu.VMEM((3, whole, nodes), F32),
            pltpu.VMEM((CHUNKS, whole, nodes), F32),
            pltpu.VMEM((CHUNKS, GROUPS, 2, pair, nodes), BF16),
            pltpu.VMEM((CHUNKS, 2, GROUPS, pair, nodes), BF16),
            pltpu.VMEM((GROUPS, pair, nodes), BF16),
            pltpu.VMEM((CHUNKS, GROUPS, pair, nodes), F32),
            pltpu.VMEM((CHUNKS, whole, nodes), F32),
            pltpu.VMEM((GROUPS, pair, nodes), BF16),
            pltpu.VMEM((GROUPS, pair, nodes), BF16),
            pltpu.SemaphoreType.DMA((14, CHUNKS)),
            pltpu.SemaphoreType.DMA((14, CHUNKS)),
            pltpu.SemaphoreType.DMA((3 + 2 * CHUNKS,)),
        ],
        compiler_params=pltpu.CompilerParams(collective_id=0, has_side_effects=True),
    )(
        fields.reshape(2 * points, rhs, nodes),
        impedance.reshape(2 * points, nodes),
        jnp.transpose(tile_cols, (2, 1, 0)),
        tile_count.reshape(modes),
        tile_data.reshape(modes, slots, 2, block, block),
        tables,
    )
    return fields + out.reshape(fields.shape)


def solution(mesh):
    placed = (
        P(None, "az", None, "curve"),
        P(None, "az", "curve"),
        P("az", "curve", None, None, None, None),
        P("az", "curve", None),
        P("az", "curve"),
    )

    def apply(*arrays):
        tables = jnp.asarray(transform_tables())
        return jax.shard_map(
            on_device,
            mesh=mesh,
            in_specs=(P(),) + placed,
            out_specs=P(None, "az", None, "curve"),
            check_vma=False,
        )(tables, *arrays)

    return apply
```

time: 72.1 us -> 63.1 us (0.88)
  the two profiles are of different devices: /device:TPU:65 before, /device:TPU:1 now
where the time goes in v2:
time: 63.1 us; the launch traced here: 63 us
  Pallas kernels  62.2 us (99%)
  other arithmetic  0.74 us (1%)
    pallas_call x1, Pallas kernels, on_device(): pl.pallas_call(kernel, out_shape=pltpu.VMEM((2 * points, rhs, nodes), F32...  62.2 us

profile of v2, /device:TPU:1, one launch (start us, length us, event | category | flops | bytes accessed | tf_op | source)
XLA Modules:
  0.0 63.0 jit_solution(8808501247325072088)
XLA Ops:
  0.0 0.0 copy-start
  0.0 62.2 %shard_map.64 = f32[32,16,128]{2,1,0:T(8,128)S(1)} custom-call(f32[32,16,128]{2,1,0:T(8,128)} %bitcast.8, f32[32,128]{1,0:T(8,128)} %bitcast.9, s32[3,1,16]{2,1,0:T(1,128)} %bitcast.10, s32[16]{0:T(128)} %bitcast.11, bf16[16,3,2,128,128]{4,3,2,1,0:T(8,128)(2,1)} %bitcast.7, bf16[2,2,256,512]{3,2,1,0:T(8,128)(2,1)} %constant.2.clone.tables_hbm), custom_call_target="tpu_custom_call" | custom-call | tf_op jit(solution)/shard_map/pallas_call | solution.py:414
  62.2 0.0 copy-done
  62.2 0.7 %add.3 = f32[2,16,16,128]{3,2,1,0:T(8,128)} add(f32[2,16,16,128]{3,2,1,0:T(8,128)S(1)} %copy-done, f32[2,16,16,128]{3,2,1,0:T(8,128)S(1)} %bitcast.6) | non-fusion elementwise | flops 65536 | bytes 786432 | tf_op jit(solution)/shard_map/add | solution.py:455
Async XLA Ops:
  0.0 62.2 %copy-start = (f32[2,16,16,128]{3,2,1,0:T(8,128)S(1)}, f32[2,16,16,128]{3,2,1,0:T(8,128)}, u32[]{:S(2)}) copy-start(f32[2,16,16,128]{3,2,1,0:T(8,128)} %param.6) | copy-start | bytes 786436

commit v3 on v2

--- a/solution.py
+++ b/solution.py
@@ -12,8 +12,8 @@
 MESH = pl.DeviceIdType.MESH
 F32 = jnp.float32
 BF16 = jnp.bfloat16
-FIELD, FIELD_OTHER, MODE_OWN, MODE_OTHER, PART, FAR_PART, WRAP_PART, WRAP_FAR = range(8)
-HALO_UP, HALO_DOWN, NEAR_SAME, NEAR_OTHER, BACK, BACK_FAR = range(8, 14)
+FIELD, FIELD_OTHER, MODE_OWN, PART, FAR_PART = range(5)
+HALO_UP, HALO_DOWN, NEAR_SAME, NEAR_OTHER, BACK, BACK_FAR = range(5, 11)
 CHUNKS = 2
 GROUPS = 8
 LOCAL = 16
@@ -69,6 +69,7 @@
     field_same,
     field_other,
     modes,
+    closing,
     part,
     far_part,
     part_in,
@@ -96,20 +97,38 @@
     far = (1 - half) * GROUPS
     last = blocks - 1
     at_end = jnp.logical_or(curve == 0, curve == last)
-    across = (az + GROUPS) % (2 * GROUPS)
-    up = (jnp.where(curve == last, across, az), (curve + 1) % blocks)
-    down = (jnp.where(curve == 0, across, az), (curve + last) % blocks)
-    up_source = jnp.where(curve == last, 3, 1)
-    down_source = jnp.where(curve == 0, 3, 1)
+    up = (az, (curve + 1) % blocks)
+    down = (az, (curve + last) % blocks)
+    beyond = jnp.where(curve == 0, last, 0)
+    beyond_place = jnp.where(curve == 0, 2, 0)
+    beyond_row = jnp.where(curve == 0, HALO_DOWN, HALO_UP)
 
     def peer(step):
         return (me + step) % GROUPS
 
     barrier = pltpu.get_barrier_semaphore()
-    greeted = [(far + peer(step), curve) for step in range(GROUPS)]
-    greeted += [up, down] + [(base + peer(step), curve) for step in range(1, GROUPS)]
-    for device in greeted:
+
+    def greet(device):
         pl.semaphore_signal(barrier, inc=1, device_id=device, device_id_type=MESH)
+
+    for step in range(GROUPS):
+        greet((far + peer(step), curve))
+
+    @pl.when(at_end)
+    def _():
+        for step in range(GROUPS):
+            greet((far + peer(step), beyond))
+
+    @pl.when(curve != last)
+    def _():
+        greet(up)
+
+    @pl.when(curve != 0)
+    def _():
+        greet(down)
+
+    for step in range(1, GROUPS):
+        greet((base + peer(step), curve))
 
     def field_load(chunk):
         rows = pl.ds(chunk * GROUPS, GROUPS)
@@ -179,83 +198,75 @@
 
     fill(0)
     fill(1)
-    pl.semaphore_wait(barrier, len(greeted))
-    send_other(stage, field_other, FIELD_OTHER, 0)
+    pl.semaphore_wait(barrier, jnp.where(at_end, 3 * GROUPS, 2 * GROUPS + 1))
+    send_other(stage, field_other.at[0], FIELD_OTHER, 0)
     send_same(stage, field_same, FIELD, 1)
+
+    @pl.when(at_end)
+    def _():
+        send_other(stage, field_other.at[1], FIELD_OTHER, 1)
+
     send_same(stage, field_same, FIELD, 0)
     table_load.wait()
 
-    def send_far(kind, row, chunk):
-        for step in range(GROUPS):
-            group = peer(step)
-            remote(far_part.at[chunk, kind, group], far_in.at[chunk, kind, me], row, chunk, (far + group, curve))
-
-    def send_near(kind, row, chunk):
-        for step in range(1, GROUPS):
-            group = peer(step)
-            remote(part.at[chunk, kind, group], part_in.at[chunk, kind, me], row, chunk, (base + group, curve))
-        part_in[chunk, kind, me] = part[chunk, kind, me]
-
     scale = 1.0 / (2 * GROUPS * LOCAL)
 
-    def send_modes(total, kind, place, row, chunk):
-        modes[kind] = (total * scale).astype(BF16).reshape(modes.shape[1:])
-        for step in range(1, GROUPS):
-            group = peer(step)
-            remote(modes.at[kind, group], window.at[chunk, place, me], row, chunk, (base + group, curve))
-        window[chunk, place, me] = modes[kind, me]
+    def settled(total):
+        return (total * scale).astype(BF16)
 
     def forward_first(chunk):
         take(field_same.at[chunk, :, pl.ds(0, GROUPS - 1)], FIELD, chunk)
         total = transform_same(field_same, chunk, half, 0)
-        take(field_other, FIELD_OTHER, chunk)
-        send_modes(total + transform_other(field_other, half, 1), 0, 1, MODE_OWN, chunk)
-
-        @pl.when(at_end)
-        def _():
-            wrapped = transform_same(field_same, chunk, 1 - half, 1) + transform_other(field_other, 1 - half, 0)
-            send_modes(wrapped, 1, 3, MODE_OTHER, chunk)
+        take(field_other.at[chunk], FIELD_OTHER, chunk)
+        total = total + transform_other(field_other.at[chunk], half, 1)
+        modes[...] = settled(total).reshape(modes.shape)
+        for step in range(1, GROUPS):
+            group = peer(step)
+            remote(modes.at[group], window.at[chunk, 1, me], MODE_OWN, chunk, (base + group, curve))
+        window[chunk, 1, me] = modes[me]
 
     def forward_last(chunk):
         take(field_same.at[chunk, :, pl.ds(0, GROUPS - 1)], FIELD, chunk)
         theirs = transform_same(field_same, chunk, 1 - half, 1)
-        far_part[chunk, 0] = theirs.astype(BF16).reshape(far_part.shape[2:])
-        send_far(0, FAR_PART, chunk)
+        far_part[...] = theirs.astype(BF16).reshape(far_part.shape)
+        for step in range(GROUPS):
+            group = peer(step)
+            remote(far_part.at[group], far_in.at[me], FAR_PART, chunk, (far + group, curve))
         ours = transform_same(field_same, chunk, half, 0)
-        part[chunk, 0] = ours.reshape(part.shape[2:])
-        send_near(0, PART, chunk)
-
+        part[...] = ours.reshape(part.shape)
+        for step in range(1, GROUPS):
+            group = peer(step)
+            remote(part.at[group], part_in.at[me], PART, chunk, (base + group, curve))
+        part_in[me] = part[me]
+
+    def close(chunk):
         @pl.when(at_end)
         def _():
-            far_part[chunk, 1] = part[chunk, 0].astype(BF16)
-            send_far(1, WRAP_FAR, chunk)
-            part[chunk, 1] = theirs.reshape(part.shape[2:])
-            send_near(1, WRAP_PART, chunk)
-
-    def settle(chunk, kind, place):
-        total = part_in[chunk, kind] + far_in[chunk, kind].astype(F32)
-        window[chunk, place] = (total * scale).astype(BF16)
+            if chunk == 1:
+                take(field_other.at[chunk], FIELD_OTHER, chunk)
+            total = transform_same(field_same, chunk, 1 - half, 1)
+            total = total + transform_other(field_other.at[chunk], 1 - half, 0)
+            closing[chunk] = settled(total).reshape(closing.shape[1:])
+            for step in range(GROUPS):
+                group = peer(step)
+                target = window.at[chunk, beyond_place, me]
+                remote(closing.at[chunk, group], target, beyond_row, chunk, (far + group, beyond))
 
     def halo(chunk):
         if chunk == 0:
             take(window.at[chunk, 1, pl.ds(0, GROUPS - 1)], MODE_OWN, chunk)
-
-            @pl.when(at_end)
-            def _():
-                take(window.at[chunk, 3, pl.ds(0, GROUPS - 1)], MODE_OTHER, chunk)
         else:
-            take(part_in.at[chunk, 0, pl.ds(0, GROUPS - 1)], PART, chunk)
-            take(far_in.at[chunk, 0], FAR_PART, chunk)
-            settle(chunk, 0, 1)
-
-            @pl.when(at_end)
-            def _():
-                take(part_in.at[chunk, 1, pl.ds(0, GROUPS - 1)], WRAP_PART, chunk)
-                take(far_in.at[chunk, 1], WRAP_FAR, chunk)
-                settle(chunk, 1, 3)
-
-        remote(window.at[chunk, up_source], window.at[chunk, 0], HALO_UP, chunk, up)
-        remote(window.at[chunk, down_source], window.at[chunk, 2], HALO_DOWN, chunk, down)
+            take(part_in.at[pl.ds(0, GROUPS - 1)], PART, chunk)
+            take(far_in, FAR_PART, chunk)
+            window[chunk, 1] = settled(part_in[...] + far_in[...].astype(F32))
+
+        @pl.when(curve != last)
+        def _():
+            remote(window.at[chunk, 1], window.at[chunk, 0], HALO_UP, chunk, up)
+
+        @pl.when(curve != 0)
+        def _():
+            remote(window.at[chunk, 1], window.at[chunk, 2], HALO_DOWN, chunk, down)
 
     def slot_of(mode, place):
         block = (curve + place + last) % blocks
@@ -368,7 +379,9 @@
     tile_load.wait()
     prepare()
     forward_first(0)
+    close(0)
     halo(0)
+    close(1)
     halo(1)
     near_own(0)
     near_own(1)
@@ -379,16 +392,14 @@
     combine(0)
     combine(1)
 
-    drain(field_other, FIELD_OTHER, 0)
+    drain(field_other.at[0], FIELD_OTHER, 0)
     drain(window.at[0, 1, pl.ds(0, GROUPS - 1)], MODE_OWN, 0)
-    drain(far_in.at[1, 0], FAR_PART, 1)
-    drain(part_in.at[1, 0, pl.ds(0, GROUPS - 1)], PART, 1)
+    drain(far_in, FAR_PART, 1)
+    drain(part_in.at[pl.ds(0, GROUPS - 1)], PART, 1)
 
     @pl.when(at_end)
     def _():
-        drain(window.at[0, 3, pl.ds(0, GROUPS - 1)], MODE_OTHER, 0)
-        drain(far_in.at[1, 1], WRAP_FAR, 1)
-        drain(part_in.at[1, 1, pl.ds(0, GROUPS - 1)], WRAP_PART, 1)
+        drain(field_other.at[1], FIELD_OTHER, 1)
 
     for chunk in range(CHUNKS):
         drain(field_same.at[chunk, :, pl.ds(0, GROUPS - 1)], FIELD, chunk)
@@ -423,13 +434,14 @@
             pltpu.VMEM(tables.shape, BF16),
             pltpu.VMEM((CHUNKS, GROUPS, 2, pair, nodes), BF16),
             pltpu.VMEM((CHUNKS, 2, GROUPS, pair, nodes), BF16),
-            pltpu.VMEM((GROUPS, pair, nodes), BF16),
-            pltpu.VMEM((2, GROUPS, pair, nodes), BF16),
-            pltpu.VMEM((CHUNKS, 2, GROUPS, pair, nodes), F32),
-            pltpu.VMEM((CHUNKS, 2, GROUPS, pair, nodes), BF16),
-            pltpu.VMEM((CHUNKS, 2, GROUPS, pair, nodes), F32),
-            pltpu.VMEM((CHUNKS, 2, GROUPS, pair, nodes), BF16),
-            pltpu.VMEM((CHUNKS, 4, GROUPS, pair, nodes), BF16),
+            pltpu.VMEM((CHUNKS, GROUPS, pair, nodes), BF16),
+            pltpu.VMEM((GROUPS, pair, nodes), BF16),
+            pltpu.VMEM((CHUNKS, GROUPS, pair, nodes), BF16),
+            pltpu.VMEM((GROUPS, pair, nodes), F32),
+            pltpu.VMEM((GROUPS, pair, nodes), BF16),
+            pltpu.VMEM((GROUPS, pair, nodes), F32),
+            pltpu.VMEM((GROUPS, pair, nodes), BF16),
+            pltpu.VMEM((CHUNKS, 3, GROUPS, pair, nodes), BF16),
             pltpu.VMEM((3, whole, nodes), F32),
             pltpu.VMEM((CHUNKS, whole, nodes), F32),
             pltpu.VMEM((CHUNKS, GROUPS, 2, pair, nodes), BF16),
@@ -439,8 +451,8 @@
             pltpu.VMEM((CHUNKS, whole, nodes), F32),
             pltpu.VMEM((GROUPS, pair, nodes), BF16),
             pltpu.VMEM((GROUPS, pair, nodes), BF16),
-            pltpu.SemaphoreType.DMA((14, CHUNKS)),
-            pltpu.SemaphoreType.DMA((14, CHUNKS)),
+            pltpu.SemaphoreType.DMA((11, CHUNKS)),
+            pltpu.SemaphoreType.DMA((11, CHUNKS)),
             pltpu.SemaphoreType.DMA((3 + 2 * CHUNKS,)),
         ],
         compiler_params=pltpu.CompilerParams(collective_id=0, has_side_effects=True),

time: 63.1 us -> 60.9 us (0.965)
  the two profiles are of different devices: /device:TPU:1 before, /device:TPU:33 now
where the time goes in v3:
time: 60.9 us; the launch traced here: 60.7 us
  Pallas kernels  60 us (99%)
  other arithmetic  0.74 us (1%)
    pallas_call x1, Pallas kernels, on_device(): pl.pallas_call(kernel, out_shape=pltpu.VMEM((2 * points, rhs, nodes), F32...  60 us

profile of v3, /device:TPU:33, one launch (start us, length us, event | category | flops | bytes accessed | tf_op | source)
XLA Modules:
  0.0 60.7 jit_solution(17995805841280555730)
XLA Ops:
  0.0 0.0 copy-start
  0.0 60.0 %shard_map.64 = f32[32,16,128]{2,1,0:T(8,128)S(1)} custom-call(f32[32,16,128]{2,1,0:T(8,128)} %bitcast.8, f32[32,128]{1,0:T(8,128)} %bitcast.9, s32[3,1,16]{2,1,0:T(1,128)} %bitcast.10, s32[16]{0:T(128)} %bitcast.11, bf16[16,3,2,128,128]{4,3,2,1,0:T(8,128)(2,1)} %bitcast.7, bf16[2,2,256,512]{3,2,1,0:T(8,128)(2,1)} %constant.2.clone.tables_hbm), custom_call_target="tpu_custom_call" | custom-call | tf_op jit(solution)/shard_map/pallas_call | solution.py:425
  60.0 0.0 copy-done
  60.0 0.7 %add.3 = f32[2,16,16,128]{3,2,1,0:T(8,128)} add(f32[2,16,16,128]{3,2,1,0:T(8,128)S(1)} %copy-done, f32[2,16,16,128]{3,2,1,0:T(8,128)S(1)} %bitcast.6) | non-fusion elementwise | flops 65536 | bytes 786432 | tf_op jit(solution)/shard_map/add | solution.py:467
Async XLA Ops:
  0.0 60.0 %copy-start = (f32[2,16,16,128]{3,2,1,0:T(8,128)S(1)}, f32[2,16,16,128]{3,2,1,0:T(8,128)}, u32[]{:S(2)}) copy-start(f32[2,16,16,128]{3,2,1,0:T(8,128)} %param.6) | copy-start | bytes 786436

commit v4 on v3

--- a/solution.py
+++ b/solution.py
@@ -372,8 +372,8 @@
             imped_real = imped_ref[pl.ds(point, 1), :]
             imped_imag = imped_ref[pl.ds(point + LOCAL, 1), :]
             rows = pl.ds(chunk * GROUPS, GROUPS)
-            out[point, rows, :] = imped_real * real + imped_imag * minus_imag
-            out[point + LOCAL, rows, :] = imped_imag * real - imped_real * minus_imag
+            out[point, rows, :] = fields[chunk, point] + imped_real * real + imped_imag * minus_imag
+            out[point + LOCAL, rows, :] = fields[chunk, point + LOCAL] + imped_imag * real - imped_real * minus_imag
 
     forward_last(1)
     tile_load.wait()
@@ -464,7 +464,7 @@
         tile_data.reshape(modes, slots, 2, block, block),
         tables,
     )
-    return fields + out.reshape(fields.shape)
+    return out.reshape(fields.shape)
 
 
 def solution(mesh):

time: 60.9 us -> 60.8 us (level)
  other arithmetic: 0.74 us -> 0 us
  local copies, waits for them, and re-layouts: 0.01 us -> 0.71 us
    add x1 -> x0, other arithmetic: 0.74 us -> none  [on_device(): return fields + out.reshape(fields.shape)]
    unnamed x2 -> x1, local copies, waits for them, and re-layouts: 0.01 us -> 0.71 us
where the time goes in v4:
time: 60.8 us; the launch traced here: 60.5 us
  Pallas kernels  59.8 us (98%)
  local copies, waits for them, and re-layouts  0.71 us (1%)
    pallas_call x1, Pallas kernels, on_device(): pl.pallas_call(kernel, out_shape=pltpu.VMEM((2 * points, rhs, nodes), F32...  59.8 us

profile of v4, /device:TPU:33, one launch (start us, length us, event | category | flops | bytes accessed | tf_op | source)
XLA Modules:
  0.0 60.5 jit_solution(9973245762884423584)
XLA Ops:
  0.0 59.8 %shard_map.64 = f32[32,16,128]{2,1,0:T(8,128)S(1)} custom-call(f32[32,16,128]{2,1,0:T(8,128)} %bitcast.8, f32[32,128]{1,0:T(8,128)} %bitcast.9, s32[3,1,16]{2,1,0:T(1,128)} %bitcast.10, s32[16]{0:T(128)} %bitcast.11, bf16[16,3,2,128,128]{4,3,2,1,0:T(8,128)(2,1)} %bitcast.7, bf16[2,2,256,512]{3,2,1,0:T(8,128)(2,1)} %constant.2.clone.tables_hbm), custom_call_target="tpu_custom_call" | custom-call | tf_op jit(solution)/shard_map/pallas_call | solution.py:425
  59.8 0.7 %copy.8 = f32[2,16,16,128]{3,2,1,0:T(8,128)} copy(f32[2,16,16,128]{3,2,1,0:T(8,128)S(1)} %bitcast.6) | data formatting | bytes 524288
